TPU v7x, 256 devices: a whole 4x4x8 slice. The times are simulated.
256 devices in a mesh: section: 2 (over core), row: 8 (over x_hi, y), col: 16 (over z, x_lo).
Axes of the slice: x: 4 (x_hi: 2, x_lo: 2; x = x_hi * 2 + x_lo), y: 4, z: 8, core: 2. Of those that a mesh axis runs over, the one named last changes fastest.
Arguments:
- section_input: bfloat16 [128, 245760], P('row', ('section', 'col')), may hold values from -6 to 6
- cache_three: bfloat16 [128, 122880], P('row', ('section', 'col')), may hold values from -6 to 6
- gain_three: float32 [192], replicated, may hold values from 0.25 to 1.75
- bias_three: float32 [192], replicated, may hold values from -2 to 2
- weight_three: bfloat16 [27, 36864], replicated, may hold values from -0.078125 to 0.078125
- weight_up: bfloat16 [9, 18432], replicated, may hold values from -0.15625 to 0.15625
- bias_up: float32 [96], replicated, may hold values from -2 to 2
- cache_four: bfloat16 [256, 122880], P('row', ('section', 'col')), may hold values from -6 to 6
- gain_four: float32 [96], replicated, may hold values from 0.25 to 1.75
- weight_four: bfloat16 [27, 9216], replicated, may hold values from -0.125 to 0.125
- bias_four: float32 [96], replicated, may hold values from -2 to 2
Outputs:
- frame_out: bfloat16 [256, 245760], P('row', ('section', 'col'))
All inputs are finite; a program needn't handle non-finite values.
Results may differ from a plain program's by a relative error of at most 0.0085.
Values may be sent and summed in bfloat16 or wider, within the bound.
A program may use at most 64 MiB of HBM per device.

v0:
```python
import functools

import jax
import jax.numpy as jnp
from jax import lax
from jax.experimental import pallas as pl
from jax.experimental.pallas import tpu as pltpu
from jax.sharding import PartitionSpec as P

EPSILON = 1e-06
MESH = pl.DeviceIdType.MESH
BF = jnp.bfloat16
F32 = jnp.float32
C3 = 192
C4 = 96
ROWS = 16
COLS = 10
FRAMES = 4
BLOCK = 24
X_LANES = COLS * FRAMES * C3
P_LANES = COLS * 2 * C3
Q_LANES = 2 * COLS * 2 * C4
EDGE = X_LANES + P_LANES + Q_LANES
CORNER = 1536 + 768 + 256


def widen(value, lanes):
    pad = lanes - value.shape[1]
    return jnp.concatenate([value, jnp.zeros((value.shape[0], pad), value.dtype)], axis=1)


def norm_act(values, gain, channels):
    meansq = jnp.sum(values * values, axis=-1, keepdims=True) * (1.0 / channels)
    scaled = values * lax.rsqrt(meansq + EPSILON) * gain
    return scaled / (1.0 + jnp.exp(-scaled))


def rounded(values):
    return values.astype(BF).astype(F32)


def by_tap(chunk, outs, stride, take):
    taps = chunk.shape[0]
    full = -(-taps // 8) * 8
    wide = jnp.concatenate([chunk, jnp.zeros((full - taps, chunk.shape[1]), chunk.dtype)], 0).astype(F32)
    pieces = []
    for start, count in take:
        stacked = jnp.stack(
            [widen(wide[:, o * stride + start : o * stride + start + count], 128) if count < 128 else
             wide[:, o * stride + start : o * stride + start + count] for o in range(outs)], 0)
        pieces.append(jnp.swapaxes(stacked, 0, 1))
    return pieces


def kernel(
    sizes,
    x_hbm, p_hbm, q_hbm, w3_hbm, wu_hbm, w4_hbm, g3, b3, bu, g4, b4,
    out,
    xv, pv, qv, w3v, wuv, w4v,
    top, bottom, corner_send,
    from_up, from_down, corner_recv, xl, xr, pl_, pr, ql, qr,
    xs, ps, act, act_one, wt3, wtu, wt4, r3s, s4, a4, resid, qext, outs,
    load_sem, send_sem, recv_sem,
):
    row_count, section_count, col_count = sizes
    r = lax.axis_index("row")
    flat_count = section_count * col_count
    g = lax.axis_index("section") * col_count + lax.axis_index("col")
    up, down = lax.rem(r + row_count - 1, row_count), lax.rem(r + 1, row_count)
    left, right = lax.rem(g + flat_count - 1, flat_count), lax.rem(g + 1, flat_count)

    def device(row, flat):
        return {"row": row, "section": flat // col_count, "col": lax.rem(flat, col_count)}

    neighbours = [(up, left), (up, g), (up, right), (r, left), (r, right), (down, left), (down, g), (down, right)]

    loads = [
        pltpu.make_async_copy(src, dst, load_sem.at[i])
        for i, (src, dst) in enumerate(
            ((x_hbm, xv), (p_hbm, pv), (q_hbm, qv), (wu_hbm, wuv), (w4_hbm, w4v), (w3_hbm, w3v))
        )
    ]
    for load in loads:
        load.start()

    barrier = pltpu.get_barrier_semaphore()
    for row, flat in neighbours:
        pl.semaphore_signal(barrier, inc=1, device_id=device(row, flat), device_id_type=MESH)

    for load in loads[:3]:
        load.wait()
    for buf, rows3, rows4 in ((top, (0, 2), (0, 2)), (bottom, (ROWS - 2, ROWS), (2 * ROWS - 2, 2 * ROWS))):
        buf[:, 0:X_LANES] = xv[rows3[0] : rows3[1], :]
        buf[:, X_LANES : X_LANES + P_LANES] = pv[rows3[0] : rows3[1], :]
        buf[:, X_LANES + P_LANES : EDGE] = qv[rows4[0] : rows4[1], :]
    for index, (rows3, rows4, high) in enumerate(
        (
            ((0, 2), (0, 2), False),
            ((0, 2), (0, 2), True),
            ((ROWS - 2, ROWS), (2 * ROWS - 2, 2 * ROWS), False),
            ((ROWS - 2, ROWS), (2 * ROWS - 2, 2 * ROWS), True),
        )
    ):
        xo, po, qo = (X_LANES - 1536, P_LANES - 768, Q_LANES - 256) if high else (0, 0, 0)
        corner_send[index, :, 0:1536] = xv[rows3[0] : rows3[1], xo : xo + 1536]
        corner_send[index, :, 1536:2304] = pv[rows3[0] : rows3[1], po : po + 768]
        corner_send[index, :, 2304:2560] = qv[rows4[0] : rows4[1], qo : qo + 256]

    pl.semaphore_wait(barrier, len(neighbours))

    plan = [
        (top, from_down, up, g),
        (bottom, from_up, down, g),
        (corner_send.at[0], corner_recv.at[3], up, left),
        (corner_send.at[1], corner_recv.at[2], up, right),
        (corner_send.at[2], corner_recv.at[1], down, left),
        (corner_send.at[3], corner_recv.at[0], down, right),
        (xv.at[:, 0:1536], xr, r, left),
        (xv.at[:, X_LANES - 1536 : X_LANES], xl, r, right),
        (pv.at[:, 0:768], pr, r, left),
        (pv.at[:, P_LANES - 768 : P_LANES], pl_, r, right),
        (qv.at[:, 0:256], qr, r, left),
        (qv.at[:, Q_LANES - 256 : Q_LANES], ql, r, right),
    ]
    copies = [
        pltpu.make_async_remote_copy(
            src_ref=src,
            dst_ref=dst,
            send_sem=send_sem.at[i],
            recv_sem=recv_sem.at[i],
            device_id=device(row, flat),
            device_id_type=MESH,
        )
        for i, (src, dst, row, flat) in enumerate(plan)
    ]
    for copy in copies:
        copy.start()

    wt3[...] = jnp.zeros_like(wt3)
    wtu[...] = jnp.zeros_like(wtu)
    wt4[...] = jnp.zeros_like(wt4)
    xs[...] = jnp.zeros_like(xs)
    ps[...] = jnp.zeros_like(ps)
    a4[...] = jnp.zeros_like(a4)
    r3s[0:96, :] = jnp.zeros((96, 768), BF)
    r3s[13 * 96 : 14 * 96, :] = jnp.zeros((96, 768), BF)

    loads[3].wait()

    def up_weights(group, _):
        chunk = wuv[:, pl.ds(pl.multiple_of(group * 16 * C3, 128), 16 * C3)]
        pieces = by_tap(chunk, 16, C3, ((0, 128), (128, 64)))
        for half, taps in enumerate(pieces):
            tap = [[taps[3 * dy + dx] for dx in range(3)] for dy in range(3)]
            across = [
                {(0, 0): line[0], (0, 1): line[1] + line[2], (1, 1): line[0] + line[1], (1, 2): line[2]} for line in tap
            ]
            for (px, dx), _first in across[0].items():
                vals = [line[(px, dx)] for line in across]
                for py, slots in enumerate(((vals[0], vals[1] + vals[2]), (vals[0] + vals[1], vals[2]))):
                    for slot, val in enumerate(slots):
                        lane = dx * 512 + slot * 256 + half * 128
                        wtu[py, pl.ds(pl.multiple_of(px * 128 + group * 16, 16), 16), lane : lane + 128] = val.astype(BF)
        return 0

    lax.fori_loop(0, 6, up_weights, 0)

    loads[4].wait()

    def four_weights(group, _):
        chunk = w4v[:, pl.ds(pl.multiple_of(group * 16 * C4, 128), 16 * C4)]
        (taps,) = by_tap(chunk, 16, C4, ((0, C4),))
        for t in range(3):
            for dx in range(3):
                for dy in range(3):
                    val = taps[9 * t + 3 * dy + dx].astype(BF)
                    for py in range(2):
                        lane = (t * 3 + dx) * 512 + (dy + py) * 128
                        wt4[pl.ds(pl.multiple_of(py * 128 + group * 16, 16), 16), lane : lane + 128] = val
        return 0

    lax.fori_loop(0, 6, four_weights, 0)

    loads[5].wait()

    def three_weights(group, _):
        chunk = w3v[:, pl.ds(pl.multiple_of(group * 16 * C3, 128), 16 * C3)]
        pieces = by_tap(chunk, 16, C3, ((0, 128), (128, 64)))
        for half, taps in enumerate(pieces):
            for t in range(3):
                for dx in range(3):
                    for dy in range(3):
                        lane = ((t * 3 + dx) * 3 + dy) * 256 + half * 128
                        wt3[pl.ds(pl.multiple_of(group * 16, 16), 16), lane : lane + 128] = taps[
                            9 * t + 3 * dy + dx
                        ].astype(BF)
        return 0

    lax.fori_loop(0, 12, three_weights, 0)

    for copy in copies:
        copy.wait()

    at_top, at_bottom, at_left, at_right = r == 0, r == row_count - 1, g == 0, g == flat_count - 1

    def keep(value, outside):
        return jnp.where(outside, jnp.zeros_like(value), value)

    for je in range(14):
        j = je - 2
        for frames, buf, main, low, high, edge_base, corner_base in (
            (FRAMES, xs, xv, xl, xr, 0, 0),
            (2, ps, pv, pl_, pr, X_LANES, 1536),
        ):
            wide = frames * C3
            if j < 0:
                side = at_left
                mid = keep(low[:, je * wide : (je + 1) * wide].astype(F32), side)
                above = corner_recv[0, :, corner_base + je * wide : corner_base + (je + 1) * wide].astype(F32)
                below = corner_recv[2, :, corner_base + je * wide : corner_base + (je + 1) * wide].astype(F32)
            elif j >= COLS:
                side = at_right
                jr = j - COLS
                mid = keep(high[:, jr * wide : (jr + 1) * wide].astype(F32), side)
                above = corner_recv[1, :, corner_base + jr * wide : corner_base + (jr + 1) * wide].astype(F32)
                below = corner_recv[3, :, corner_base + jr * wide : corner_base + (jr + 1) * wide].astype(F32)
            else:
                side = jnp.bool_(False)
                mid = main[:, j * wide : (j + 1) * wide].astype(F32)
                above = from_up[:, edge_base + j * wide : edge_base + (j + 1) * wide].astype(F32)
                below = from_down[:, edge_base + j * wide : edge_base + (j + 1) * wide].astype(F32)
            above = keep(above, jnp.logical_or(side, at_top))
            below = keep(below, jnp.logical_or(side, at_bottom))
            for k in range(frames):
                base = (je * frames + k) * BLOCK
                lanes = slice(k * C3, (k + 1) * C3)
                buf[base : base + 16, 0:C3] = mid[:, lanes]
                buf[base + 16 : base + 18, 0:C3] = below[:, lanes]
                buf[base + 22 : base + 24, 0:C3] = above[:, lanes]

    gain3 = widen(g3[...].reshape(1, C3), 256)
    bias3 = widen(b3[...].reshape(1, C3), 256)

    def build(je, _):
        raw = xs[pl.ds(pl.multiple_of(je * 96, 32), 96), :]
        new = norm_act(raw, gain3, C3).reshape(4, BLOCK, 256)
        old = ps[pl.ds(pl.multiple_of(je * 48, 16), 48), :].reshape(2, BLOCK, 256)
        frames = jnp.concatenate([old, new], 0)
        for slot, shift in enumerate((1, 0, BLOCK - 1)):
            moved = pltpu.roll(frames, shift, axis=1) if shift else frames
            lanes = slice(slot * 256, (slot + 1) * 256)
            act[pl.ds(pl.multiple_of(je * 144, 16), 144), lanes] = moved.reshape(144, 256).astype(BF)
            act_one[pl.ds(pl.multiple_of(je * 96, 32), 96), lanes] = moved[1:5].reshape(96, 256).astype(BF)
        return 0

    lax.fori_loop(0, 14, build, 0)

    def three(chunk, _):
        parts = []
        for t in range(3):
            for dx in range(3):
                rows = []
                for j in range(4):
                    je = chunk * 4 + j + dx
                    if t == 1:
                        rows.append(act_one[pl.ds(pl.multiple_of(je * 96, 32), 96), :])
                    else:
                        rows.append(act[pl.ds(pl.multiple_of(je * 144 + 24 * t, 16), 96), :])
                parts.append(jnp.concatenate(rows, 0))
        total = lax.dot_general(
            jnp.concatenate(parts, 1), wt3[...], (((1,), (1,)), ((), ())), preferred_element_type=F32
        )
        total = xs[pl.ds(pl.multiple_of(chunk * 384 + 96, 32), 384), :] + (total + bias3)
        total = total.reshape(16, BLOCK, 256)
        blk = lax.broadcasted_iota(jnp.int32, (16, BLOCK, 256), 0) + chunk * 16
        rr = lax.broadcasted_iota(jnp.int32, (16, BLOCK, 256), 1)
        lowest = jnp.where(at_left, 4, 0)
        highest = jnp.where(at_right, 44, 48)
        up_row = jnp.where(at_top, 23, -1)
        down_row = jnp.where(at_bottom, 16, -1)
        inside = (blk >= lowest) & (blk < highest) & (rr != up_row) & (rr != down_row)
        total = rounded(jnp.where(inside, total, 0.0))
        for slot, shift in enumerate((1, 0, BLOCK - 1)):
            moved = pltpu.roll(total, shift, axis=1) if shift else total
            r3s[pl.ds(pl.multiple_of(chunk * 384 + 96, 32), 384), slot * 256 : (slot + 1) * 256] = moved.reshape(
                384, 256
            ).astype(BF)
        return 0

    lax.fori_loop(0, 3, three, 0)

    bias_u = bu[...].reshape(1, C4)
    bias_u = jnp.concatenate([widen(bias_u, 128)] * 2, 1)

    def upsample(chunk, _):
        for py in range(2):
            parts = [
                r3s[pl.ds(pl.multiple_of(chunk * 384 + dx * 96, 32), 384), py * 256 : py * 256 + 512]
                for dx in range(3)
            ]
            total = lax.dot_general(
                jnp.concatenate(parts, 1), wtu[py], (((1,), (1,)), ((), ())), preferred_element_type=F32
            )
            s4[py, pl.ds(pl.multiple_of(chunk * 384, 128), 384), :] = total + bias_u
        return 0

    lax.fori_loop(0, 3, upsample, 0)

    gain4 = widen(g4[...].reshape(1, C4), 128)

    def four_in(jj, _):
        for px in range(2):
            acts = []
            at = jj * 2 + px
            for py in range(2):
                value = rounded(s4[py, pl.ds(pl.multiple_of(jj * 96, 32), 96), px * 128 : px * 128 + 128])
                shaped = value.reshape(4, BLOCK, 128)
                resid[pl.ds(pl.multiple_of(at * 64, 64), 64), py * 128 : py * 128 + 128] = shaped[:, 0:16].reshape(64, 128)
                active = norm_act(value, gain4, C4).reshape(4, BLOCK, 128)
                rr = lax.broadcasted_iota(jnp.int32, (4, BLOCK, 128), 1)
                line = jnp.where(at_bottom, 16, -1) if py == 0 else jnp.where(at_top, 23, -1)
                column = jnp.logical_or(jnp.logical_and(at_left, at < 2), jnp.logical_and(at_right, at > 21))
                line = jnp.where(column, -2, line)
                active = jnp.where(jnp.logical_or(rr == line, line == -2), 0.0, active)
                acts.append(active)
            slots = (
                pltpu.roll(acts[1], 1, axis=1),
                acts[0],
                acts[1],
                pltpu.roll(acts[0], BLOCK - 1, axis=1),
            )
            for slot, value in enumerate(slots):
                a4[pl.ds(pl.multiple_of(at * 96 + 32, 32), 64), slot * 128 : slot * 128 + 128] = (
                    value[:, 0:16].reshape(64, 128).astype(BF)
                )
        return 0

    lax.fori_loop(0, 12, four_in, 0)

    qext[...] = jnp.zeros_like(qext)
    edge_q = X_LANES + P_LANES
    qext[0:32, 256 : 256 + Q_LANES] = qv[...]
    qext[0:32, 0:256] = keep(ql[...], at_left)
    qext[0:32, 256 + Q_LANES : 512 + Q_LANES] = keep(qr[...], at_right)
    for base, edge, outside, low_corner, high_corner in (
        (32, from_up, at_top, 0, 1),
        (40, from_down, at_bottom, 2, 3),
    ):
        qext[base : base + 2, 256 : 256 + Q_LANES] = keep(edge[:, edge_q:EDGE], outside)
        qext[base : base + 2, 0:256] = keep(corner_recv[low_corner, :, 2304:2560], jnp.logical_or(outside, at_left))
        qext[base : base + 2, 256 + Q_LANES : 512 + Q_LANES] = keep(
            corner_recv[high_corner, :, 2304:2560], jnp.logical_or(outside, at_right)
        )
    want = lax.broadcasted_iota(jnp.int32, (64, 48), 0)
    have = lax.broadcasted_iota(jnp.int32, (64, 48), 1)
    slot = want >> 4
    i = want & 15
    source = jnp.where(
        slot == 0,
        jnp.where(i == 0, 33, 2 * i - 1),
        jnp.where(slot == 1, 2 * i, jnp.where(slot == 2, 2 * i + 1, jnp.where(i == 15, 40, 2 * i + 2))),
    )
    pick = jnp.where(source == have, 1.0, 0.0).astype(BF)
    for xe in range(22):
        start = 64 + xe * 192
        low = start // 128 * 128
        picked = jnp.dot(pick, qext[:, low : low + 256], preferred_element_type=F32)
        for t in range(2):
            off = start - low + t * C4
            piece = picked[:, off : off + C4].astype(BF)
            for s in range(4):
                a4[(xe + 1) * 96 + t * 16 : (xe + 1) * 96 + t * 16 + 16, s * 128 : s * 128 + C4] = piece[
                    s * 16 : s * 16 + 16
                ]

    bias4 = widen(b4[...].reshape(1, C4), 128)
    bias4 = jnp.concatenate([bias4, bias4], 1)

    def four(chunk, _):
        parts = []
        for t in range(3):
            for dx in range(3):
                parts.append(
                    jnp.concatenate(
                        [
                            a4[pl.ds(pl.multiple_of((chunk * 5 + x + 1 + dx) * 96 + t * 16, 16), 64), :]
                            for x in range(5)
                        ],
                        0,
                    )
                )
        total = lax.dot_general(
            jnp.concatenate(parts, 1), wt4[...], (((1,), (1,)), ((), ())), preferred_element_type=F32
        )
        total = resid[pl.ds(pl.multiple_of(chunk * 320 + 128, 64), 320), :] + (total + bias4)
        for x in range(5):
            for py in range(2):
                pieces = [
                    total[x * 64 + k * 16 : x * 64 + k * 16 + 16, py * 128 : py * 128 + C4] for k in range(4)
                ]
                line = jnp.concatenate(pieces, 1)
                for tile in range(3):
                    outs[(chunk * 5 + x) * 3 + tile, pl.ds(py, 16, stride=2), :] = line[:, tile * 128 : tile * 128 + 128]
        return 0

    lax.fori_loop(0, 4, four, 0)
    for tile in range(60):
        out[:, tile * 128 : tile * 128 + 128] = outs[tile].astype(BF)


def shards(sizes, section_input, cache_three, gain_three, bias_three, weight_three, weight_up, bias_up, cache_four,
           gain_four, weight_four, bias_four):
    vmem = pl.BlockSpec(memory_space=pltpu.VMEM)
    hbm = pl.BlockSpec(memory_space=pl.ANY)
    scratch = [
        pltpu.VMEM((ROWS, X_LANES), BF),
        pltpu.VMEM((ROWS, P_LANES), BF),
        pltpu.VMEM((2 * ROWS, Q_LANES), BF),
        pltpu.VMEM((27, C3 * C3), BF),
        pltpu.VMEM((9, C3 * C4), BF),
        pltpu.VMEM((27, C4 * C4), BF),
        pltpu.VMEM((2, EDGE), BF),
        pltpu.VMEM((2, EDGE), BF),
        pltpu.VMEM((4, 2, CORNER), BF),
        pltpu.VMEM((2, EDGE), BF),
        pltpu.VMEM((2, EDGE), BF),
        pltpu.VMEM((4, 2, CORNER), BF),
        pltpu.VMEM((ROWS, 1536), BF),
        pltpu.VMEM((ROWS, 1536), BF),
        pltpu.VMEM((ROWS, 768), BF),
        pltpu.VMEM((ROWS, 768), BF),
        pltpu.VMEM((2 * ROWS, 256), BF),
        pltpu.VMEM((2 * ROWS, 256), BF),
        pltpu.VMEM((14 * 96, 256), F32),
        pltpu.VMEM((14 * 48, 256), F32),
        pltpu.VMEM((14 * 144, 768), BF),
        pltpu.VMEM((14 * 96, 768), BF),
        pltpu.VMEM((256, 27 * 256), BF),
        pltpu.VMEM((2, 256, 1536), BF),
        pltpu.VMEM((256, 9 * 512), BF),
        pltpu.VMEM((14 * 96, 768), BF),
        pltpu.VMEM((2, 1152, 256), F32),
        pltpu.VMEM((24 * 96, 512), BF),
        pltpu.VMEM((24 * 64, 256), F32),
        pltpu.VMEM((48, Q_LANES + 512), BF),
        pltpu.VMEM((60, 32, 128), F32),
        pltpu.SemaphoreType.DMA((6,)),
        pltpu.SemaphoreType.DMA((12,)),
        pltpu.SemaphoreType.DMA((12,)),
    ]
    return pl.pallas_call(
        functools.partial(kernel, sizes),
        out_shape=jax.ShapeDtypeStruct((2 * ROWS, 2 * X_LANES // 2), BF),
        in_specs=[hbm] * 6 + [vmem] * 5,
        out_specs=vmem,
        scratch_shapes=scratch,
        compiler_params=pltpu.CompilerParams(
            collective_id=0, has_side_effects=True, vmem_limit_bytes=60 * 2**20
        ),
        name="decode",
    )(section_input, cache_three, cache_four, weight_three, weight_up, weight_four, gain_three, bias_three, bias_up,
      gain_four, bias_four)


def solution(mesh):
    sizes = (mesh.shape["row"], mesh.shape["section"], mesh.shape["col"])
    tiled = P("row", ("section", "col"))
    return jax.shard_map(
        functools.partial(shards, sizes),
        mesh=mesh,
        in_specs=(tiled, tiled, P(), P(), P(), P(), P(), tiled, P(), P(), P()),
        out_specs=tiled,
        check_vma=False,
    )
```

profile of v0, /device:TPU:1, one launch (start us, length us, event | category | flops | bytes accessed | tf_op | source)
XLA Modules:
  0.0 36.9 jit_solution(6834058781670627765)
XLA Ops:
  0.0 35.0 %decode.1 = bf16[32,7680]{1,0:T(8,128)(2,1)} custom-call(bf16[16,7680]{1,0:T(8,128)(2,1)} %x_hbm.1, bf16[16,3840]{1,0:T(8,128)(2,1)} %p_hbm.1, bf16[32,3840]{1,0:T(8,128)(2,1)} %q_hbm.1, bf16[27,36864]{1,0:T(8,128)(2,1)} %w3_hbm.1, bf16[9,18432]{1,0:T(8,128)(2,1)} %wu_hbm.1, bf16[27,9216]{1,0:T(8,128)(2,1)} %w4_hbm.1, f32[192]{0:T(256)} %g3.1, f32[192]{0:T(256)} %b3.1, ...), custom_call_target="tpu_custom_call" | custom-call | tf_op jit(solution)/shard_map/decode/pallas_call | solution.py:451
  35.0 1.8 %copy.13 = bf16[32,7680]{1,0:T(8,128)(2,1)} copy(bf16[32,7680]{1,0:T(8,128)(2,1)} %decode.1) | data formatting | bytes 983040
where the time goes:
time: 37 us; the launch traced here: 36.9 us
  Pallas kernels  35 us (95%)
  local copies, waits for them, and re-layouts  1.84 us (5%)
    pallas_call x1, Pallas kernels, shards(): pl.pallas_call(functools.partial(kernel, sizes), out_shape=jax.ShapeDtype...  35 us
    unnamed x1, local copies, waits for them, and re-layouts  1.84 us

commit v1 on v0

--- a/solution.py
+++ b/solution.py
@@ -32,7 +32,8 @@
 def norm_act(values, gain, channels):
     meansq = jnp.sum(values * values, axis=-1, keepdims=True) * (1.0 / channels)
     scaled = values * lax.rsqrt(meansq + EPSILON) * gain
-    return scaled / (1.0 + jnp.exp(-scaled))
+    half = 0.5 * scaled
+    return half + half * jnp.tanh(half)
 
 
 def rounded(values):
@@ -54,8 +55,9 @@
 
 def kernel(
     sizes,
-    x_hbm, p_hbm, q_hbm, w3_hbm, wu_hbm, w4_hbm, g3, b3, bu, g4, b4,
+    x_hbm, p_hbm, q_hbm, w3_hbm, wu_hbm, w4_hbm, g3_hbm, b3_hbm, bu_hbm, g4_hbm, b4_hbm,
     out,
+    g3, b3, bu, g4, b4,
     xv, pv, qv, w3v, wuv, w4v,
     top, bottom, corner_send,
     from_up, from_down, corner_recv, xl, xr, pl_, pr, ql, qr,
@@ -77,10 +79,11 @@
     loads = [
         pltpu.make_async_copy(src, dst, load_sem.at[i])
         for i, (src, dst) in enumerate(
-            ((x_hbm, xv), (p_hbm, pv), (q_hbm, qv), (wu_hbm, wuv), (w4_hbm, w4v), (w3_hbm, w3v))
+            ((x_hbm, xv), (p_hbm, pv), (q_hbm, qv), (wu_hbm, wuv), (w4_hbm, w4v), (w3_hbm, w3v),
+             (g3_hbm, g3), (b3_hbm, b3), (bu_hbm, bu), (g4_hbm, g4), (b4_hbm, b4))
         )
     ]
-    for load in loads:
+    for load in loads[:3]:
         load.start()
 
     barrier = pltpu.get_barrier_semaphore()
@@ -105,6 +108,9 @@
         corner_send[index, :, 0:1536] = xv[rows3[0] : rows3[1], xo : xo + 1536]
         corner_send[index, :, 1536:2304] = pv[rows3[0] : rows3[1], po : po + 768]
         corner_send[index, :, 2304:2560] = qv[rows4[0] : rows4[1], qo : qo + 256]
+
+    for load in loads[3:]:
+        load.start()
 
     pl.semaphore_wait(barrier, len(neighbours))
 
@@ -198,6 +204,8 @@
 
     lax.fori_loop(0, 12, three_weights, 0)
 
+    for load in loads[6:]:
+        load.wait()
     for copy in copies:
         copy.wait()
 
@@ -413,6 +421,11 @@
     vmem = pl.BlockSpec(memory_space=pltpu.VMEM)
     hbm = pl.BlockSpec(memory_space=pl.ANY)
     scratch = [
+        pltpu.VMEM((C3,), F32),
+        pltpu.VMEM((C3,), F32),
+        pltpu.VMEM((C4,), F32),
+        pltpu.VMEM((C4,), F32),
+        pltpu.VMEM((C4,), F32),
         pltpu.VMEM((ROWS, X_LANES), BF),
         pltpu.VMEM((ROWS, P_LANES), BF),
         pltpu.VMEM((2 * ROWS, Q_LANES), BF),
@@ -444,14 +457,14 @@
         pltpu.VMEM((24 * 64, 256), F32),
         pltpu.VMEM((48, Q_LANES + 512), BF),
         pltpu.VMEM((60, 32, 128), F32),
-        pltpu.SemaphoreType.DMA((6,)),
+        pltpu.SemaphoreType.DMA((11,)),
         pltpu.SemaphoreType.DMA((12,)),
         pltpu.SemaphoreType.DMA((12,)),
     ]
     return pl.pallas_call(
         functools.partial(kernel, sizes),
         out_shape=jax.ShapeDtypeStruct((2 * ROWS, 2 * X_LANES // 2), BF),
-        in_specs=[hbm] * 6 + [vmem] * 5,
+        in_specs=[hbm] * 11,
         out_specs=vmem,
         scratch_shapes=scratch,
         compiler_params=pltpu.CompilerParams(

time: 37 us -> 35.9 us (0.970)
  Pallas kernels: 35 us -> 34 us
    pallas_call x1, Pallas kernels: 35 us -> 34 us  [shards(): pl.pallas_call(functools.partial(kernel, sizes), out_shape=jax.ShapeDtype...]
where the time goes in v1:
time: 35.9 us; the launch traced here: 35.8 us
  Pallas kernels  34 us (95%)
  local copies, waits for them, and re-layouts  1.84 us (5%)
    pallas_call x1, Pallas kernels, shards(): pl.pallas_call(functools.partial(kernel, sizes), out_shape=jax.ShapeDtype...  34 us
    unnamed x1, local copies, waits for them, and re-layouts  1.84 us

profile of v1, /device:TPU:1, one launch (start us, length us, event | category | flops | bytes accessed | tf_op | source)
XLA Modules:
  0.0 35.8 jit_solution(5403642823684862556)
XLA Ops:
  0.0 34.0 %decode.1 = bf16[32,7680]{1,0:T(8,128)(2,1)} custom-call(bf16[16,7680]{1,0:T(8,128)(2,1)} %x_hbm.1, bf16[16,3840]{1,0:T(8,128)(2,1)} %p_hbm.1, bf16[32,3840]{1,0:T(8,128)(2,1)} %q_hbm.1, bf16[27,36864]{1,0:T(8,128)(2,1)} %w3_hbm.1, bf16[9,18432]{1,0:T(8,128)(2,1)} %wu_hbm.1, bf16[27,9216]{1,0:T(8,128)(2,1)} %w4_hbm.1, f32[192]{0:T(256)} %g3_hbm.1, ...), custom_call_target="tpu_custom_call" | custom-call | tf_op jit(solution)/shard_map/decode/pallas_call | solution.py:464
  34.0 1.8 %copy.13 = bf16[32,7680]{1,0:T(8,128)(2,1)} copy(bf16[32,7680]{1,0:T(8,128)(2,1)} %decode.1) | data formatting | bytes 983040

commit v2 on v1

--- a/solution.py
+++ b/solution.py
@@ -61,7 +61,7 @@
     xv, pv, qv, w3v, wuv, w4v,
     top, bottom, corner_send,
     from_up, from_down, corner_recv, xl, xr, pl_, pr, ql, qr,
-    xs, ps, act, act_one, wt3, wtu, wt4, r3s, s4, a4, resid, qext, outs,
+    xs, ps, an, act, act_one, wt3, wtu, wt4, r3s, s4, a4, resid, qext, outs,
     load_sem, send_sem, recv_sem,
 ):
     row_count, section_count, col_count = sizes
@@ -74,7 +74,17 @@
     def device(row, flat):
         return {"row": row, "section": flat // col_count, "col": lax.rem(flat, col_count)}
 
-    neighbours = [(up, left), (up, g), (up, right), (r, left), (r, right), (down, left), (down, g), (down, right)]
+    at_top, at_bottom, at_left, at_right = r == 0, r == row_count - 1, g == 0, g == flat_count - 1
+    has_up, has_down, has_left, has_right = r > 0, r < row_count - 1, g > 0, g < flat_count - 1
+    up_left, up_right = jnp.logical_and(has_up, has_left), jnp.logical_and(has_up, has_right)
+    down_left, down_right = jnp.logical_and(has_down, has_left), jnp.logical_and(has_down, has_right)
+
+    neighbours = [
+        (up, left, up_left), (up, g, has_up), (up, right, up_right), (r, left, has_left), (r, right, has_right),
+        (down, left, down_left), (down, g, has_down), (down, right, down_right),
+    ]
+    count_rows = jnp.where(at_top, 0, 1) + jnp.where(at_bottom, 0, 1)
+    count_cols = jnp.where(at_left, 0, 1) + jnp.where(at_right, 0, 1)
 
     loads = [
         pltpu.make_async_copy(src, dst, load_sem.at[i])
@@ -87,8 +97,11 @@
         load.start()
 
     barrier = pltpu.get_barrier_semaphore()
-    for row, flat in neighbours:
-        pl.semaphore_signal(barrier, inc=1, device_id=device(row, flat), device_id_type=MESH)
+    for row, flat, there in neighbours:
+
+        @pl.when(there)
+        def _(row=row, flat=flat):
+            pl.semaphore_signal(barrier, inc=1, device_id=device(row, flat), device_id_type=MESH)
 
     for load in loads[:3]:
         load.wait()
@@ -112,35 +125,42 @@
     for load in loads[3:]:
         load.start()
 
-    pl.semaphore_wait(barrier, len(neighbours))
+    pl.semaphore_wait(barrier, (1 + count_rows) * (1 + count_cols) - 1)
 
     plan = [
-        (top, from_down, up, g),
-        (bottom, from_up, down, g),
-        (corner_send.at[0], corner_recv.at[3], up, left),
-        (corner_send.at[1], corner_recv.at[2], up, right),
-        (corner_send.at[2], corner_recv.at[1], down, left),
-        (corner_send.at[3], corner_recv.at[0], down, right),
-        (xv.at[:, 0:1536], xr, r, left),
-        (xv.at[:, X_LANES - 1536 : X_LANES], xl, r, right),
-        (pv.at[:, 0:768], pr, r, left),
-        (pv.at[:, P_LANES - 768 : P_LANES], pl_, r, right),
-        (qv.at[:, 0:256], qr, r, left),
-        (qv.at[:, Q_LANES - 256 : Q_LANES], ql, r, right),
+        (top, from_down, up, g, has_up, has_down),
+        (bottom, from_up, down, g, has_down, has_up),
+        (xv.at[:, 0:1536], xr, r, left, has_left, has_right),
+        (xv.at[:, X_LANES - 1536 : X_LANES], xl, r, right, has_right, has_left),
+        (pv.at[:, 0:768], pr, r, left, has_left, has_right),
+        (pv.at[:, P_LANES - 768 : P_LANES], pl_, r, right, has_right, has_left),
+        (corner_send.at[0], corner_recv.at[3], up, left, up_left, down_right),
+        (corner_send.at[1], corner_recv.at[2], up, right, up_right, down_left),
+        (corner_send.at[2], corner_recv.at[1], down, left, down_left, up_right),
+        (corner_send.at[3], corner_recv.at[0], down, right, down_right, up_left),
+        (qv.at[:, 0:256], qr, r, left, has_left, has_right),
+        (qv.at[:, Q_LANES - 256 : Q_LANES], ql, r, right, has_right, has_left),
     ]
     copies = [
-        pltpu.make_async_remote_copy(
-            src_ref=src,
-            dst_ref=dst,
-            send_sem=send_sem.at[i],
-            recv_sem=recv_sem.at[i],
-            device_id=device(row, flat),
-            device_id_type=MESH,
+        (
+            pltpu.make_async_remote_copy(
+                src_ref=src,
+                dst_ref=dst,
+                send_sem=send_sem.at[i],
+                recv_sem=recv_sem.at[i],
+                device_id=device(row, flat),
+                device_id_type=MESH,
+            ),
+            sends,
+            gets,
         )
-        for i, (src, dst, row, flat) in enumerate(plan)
+        for i, (src, dst, row, flat, sends, gets) in enumerate(plan)
     ]
-    for copy in copies:
-        copy.start()
+    for copy, sends, _gets in copies:
+
+        @pl.when(sends)
+        def _(copy=copy):
+            copy.start()
 
     wt3[...] = jnp.zeros_like(wt3)
     wtu[...] = jnp.zeros_like(wtu)
@@ -206,10 +226,32 @@
 
     for load in loads[6:]:
         load.wait()
-    for copy in copies:
-        copy.wait()
-
-    at_top, at_bottom, at_left, at_right = r == 0, r == row_count - 1, g == 0, g == flat_count - 1
+
+    qext[...] = jnp.zeros_like(qext)
+    qext[0:32, 256 : 256 + Q_LANES] = qv[...]
+    gain3 = widen(g3[...].reshape(1, C3), 256)
+    bias3 = widen(b3[...].reshape(1, C3), 256)
+
+    for je in range(2, 2 + COLS):
+        for frames, buf, main in ((FRAMES, xs, xv), (2, ps, pv)):
+            wide = frames * C3
+            mid = main[:, (je - 2) * wide : (je - 1) * wide].astype(F32)
+            for k in range(frames):
+                base = (je * frames + k) * BLOCK
+                buf[base : base + 16, 0:C3] = mid[:, k * C3 : (k + 1) * C3]
+
+    def own(j, _):
+        rows = [xs[pl.ds(pl.multiple_of(j * 96 + 192 + k * BLOCK, 8), 16), :] for k in range(FRAMES)]
+        an[pl.ds(pl.multiple_of(j * 64, 64), 64), :] = norm_act(jnp.concatenate(rows, 0), gain3, C3)
+        return 0
+
+    lax.fori_loop(0, COLS, own, 0)
+
+    for copy, sends, gets in copies:
+
+        @pl.when(gets)
+        def _(copy=copy):
+            copy.wait_recv()
 
     def keep(value, outside):
         return jnp.where(outside, jnp.zeros_like(value), value)
@@ -234,7 +276,7 @@
                 below = corner_recv[3, :, corner_base + jr * wide : corner_base + (jr + 1) * wide].astype(F32)
             else:
                 side = jnp.bool_(False)
-                mid = main[:, j * wide : (j + 1) * wide].astype(F32)
+                mid = None
                 above = from_up[:, edge_base + j * wide : edge_base + (j + 1) * wide].astype(F32)
                 below = from_down[:, edge_base + j * wide : edge_base + (j + 1) * wide].astype(F32)
             above = keep(above, jnp.logical_or(side, at_top))
@@ -242,16 +284,12 @@
             for k in range(frames):
                 base = (je * frames + k) * BLOCK
                 lanes = slice(k * C3, (k + 1) * C3)
-                buf[base : base + 16, 0:C3] = mid[:, lanes]
+                if mid is not None:
+                    buf[base : base + 16, 0:C3] = mid[:, lanes]
                 buf[base + 16 : base + 18, 0:C3] = below[:, lanes]
                 buf[base + 22 : base + 24, 0:C3] = above[:, lanes]
 
-    gain3 = widen(g3[...].reshape(1, C3), 256)
-    bias3 = widen(b3[...].reshape(1, C3), 256)
-
-    def build(je, _):
-        raw = xs[pl.ds(pl.multiple_of(je * 96, 32), 96), :]
-        new = norm_act(raw, gain3, C3).reshape(4, BLOCK, 256)
+    def place(je, new):
         old = ps[pl.ds(pl.multiple_of(je * 48, 16), 48), :].reshape(2, BLOCK, 256)
         frames = jnp.concatenate([old, new], 0)
         for slot, shift in enumerate((1, 0, BLOCK - 1)):
@@ -259,9 +297,23 @@
             lanes = slice(slot * 256, (slot + 1) * 256)
             act[pl.ds(pl.multiple_of(je * 144, 16), 144), lanes] = moved.reshape(144, 256).astype(BF)
             act_one[pl.ds(pl.multiple_of(je * 96, 32), 96), lanes] = moved[1:5].reshape(96, 256).astype(BF)
-        return 0
-
-    lax.fori_loop(0, 14, build, 0)
+
+    def side_build(i, _):
+        je = i + (i // 2) * 10
+        raw = xs[pl.ds(pl.multiple_of(je * 96, 32), 96), :]
+        place(je, norm_act(raw, gain3, C3).reshape(4, BLOCK, 256))
+        return 0
+
+    def own_build(j, _):
+        je = j + 2
+        rows = [xs[pl.ds(pl.multiple_of(je * 96 + k * BLOCK + 16, 8), 8), :] for k in range(FRAMES)]
+        edge = norm_act(jnp.concatenate(rows, 0), gain3, C3).reshape(4, 8, 256)
+        main = an[pl.ds(pl.multiple_of(j * 64, 64), 64), :].reshape(4, 16, 256)
+        place(je, jnp.concatenate([main, edge], 1))
+        return 0
+
+    lax.fori_loop(0, 4, side_build, 0)
+    lax.fori_loop(0, COLS, own_build, 0)
 
     def three(chunk, _):
         parts = []
@@ -345,9 +397,7 @@
 
     lax.fori_loop(0, 12, four_in, 0)
 
-    qext[...] = jnp.zeros_like(qext)
     edge_q = X_LANES + P_LANES
-    qext[0:32, 256 : 256 + Q_LANES] = qv[...]
     qext[0:32, 0:256] = keep(ql[...], at_left)
     qext[0:32, 256 + Q_LANES : 512 + Q_LANES] = keep(qr[...], at_right)
     for base, edge, outside, low_corner, high_corner in (
@@ -412,6 +462,12 @@
         return 0
 
     lax.fori_loop(0, 4, four, 0)
+    for copy, sends, _gets in copies:
+
+        @pl.when(sends)
+        def _(copy=copy):
+            copy.wait_send()
+
     for tile in range(60):
         out[:, tile * 128 : tile * 128 + 128] = outs[tile].astype(BF)
 
@@ -446,6 +502,7 @@
         pltpu.VMEM((2 * ROWS, 256), BF),
         pltpu.VMEM((14 * 96, 256), F32),
         pltpu.VMEM((14 * 48, 256), F32),
+        pltpu.VMEM((COLS * 64, 256), F32),
         pltpu.VMEM((14 * 144, 768), BF),
         pltpu.VMEM((14 * 96, 768), BF),
         pltpu.VMEM((256, 27 * 256), BF),

time: 35.9 us -> 34.1 us (0.950)
  Pallas kernels: 34 us -> 32.1 us
    pallas_call x1, Pallas kernels: 34 us -> 32.1 us  [shards(): pl.pallas_call(functools.partial(kernel, sizes), out_shape=jax.ShapeDtype...]
where the time goes in v2:
time: 34.1 us; the launch traced here: 34 us
  Pallas kernels  32.1 us (94%)
  local copies, waits for them, and re-layouts  1.84 us (5%)
    pallas_call x1, Pallas kernels, shards(): pl.pallas_call(functools.partial(kernel, sizes), out_shape=jax.ShapeDtype...  32.1 us
    unnamed x1, local copies, waits for them, and re-layouts  1.84 us

profile of v2, /device:TPU:1, one launch (start us, length us, event | category | flops | bytes accessed | tf_op | source)
XLA Modules:
  0.0 34.0 jit_solution(10586609115457552780)
XLA Ops:
  0.0 32.1 %decode.1 = bf16[32,7680]{1,0:T(8,128)(2,1)} custom-call(bf16[16,7680]{1,0:T(8,128)(2,1)} %x_hbm.1, bf16[16,3840]{1,0:T(8,128)(2,1)} %p_hbm.1, bf16[32,3840]{1,0:T(8,128)(2,1)} %q_hbm.1, bf16[27,36864]{1,0:T(8,128)(2,1)} %w3_hbm.1, bf16[9,18432]{1,0:T(8,128)(2,1)} %wu_hbm.1, bf16[27,9216]{1,0:T(8,128)(2,1)} %w4_hbm.1, f32[192]{0:T(256)} %g3_hbm.1, ...), custom_call_target="tpu_custom_call" | custom-call | tf_op jit(solution)/shard_map/decode/pallas_call | solution.py:521
  32.1 1.8 %copy.13 = bf16[32,7680]{1,0:T(8,128)(2,1)} copy(bf16[32,7680]{1,0:T(8,128)(2,1)} %decode.1) | data formatting | bytes 983040

commit v3 on v2

--- a/solution.py
+++ b/solution.py
@@ -247,16 +247,17 @@
 
     lax.fori_loop(0, COLS, own, 0)
 
-    for copy, sends, gets in copies:
-
-        @pl.when(gets)
-        def _(copy=copy):
-            copy.wait_recv()
+    def arrive(group):
+        for copy, _sends, gets in group:
+
+            @pl.when(gets)
+            def _(copy=copy):
+                copy.wait_recv()
 
     def keep(value, outside):
         return jnp.where(outside, jnp.zeros_like(value), value)
 
-    for je in range(14):
+    def edges(je):
         j = je - 2
         for frames, buf, main, low, high, edge_base, corner_base in (
             (FRAMES, xs, xv, xl, xr, 0, 0),
@@ -312,16 +313,13 @@
         place(je, jnp.concatenate([main, edge], 1))
         return 0
 
-    lax.fori_loop(0, 4, side_build, 0)
-    lax.fori_loop(0, COLS, own_build, 0)
-
-    def three(chunk, _):
+    def three(cols):
         parts = []
         for t in range(3):
             for dx in range(3):
                 rows = []
-                for j in range(4):
-                    je = chunk * 4 + j + dx
+                for c in cols:
+                    je = c + dx
                     if t == 1:
                         rows.append(act_one[pl.ds(pl.multiple_of(je * 96, 32), 96), :])
                     else:
@@ -330,24 +328,23 @@
         total = lax.dot_general(
             jnp.concatenate(parts, 1), wt3[...], (((1,), (1,)), ((), ())), preferred_element_type=F32
         )
-        total = xs[pl.ds(pl.multiple_of(chunk * 384 + 96, 32), 384), :] + (total + bias3)
-        total = total.reshape(16, BLOCK, 256)
-        blk = lax.broadcasted_iota(jnp.int32, (16, BLOCK, 256), 0) + chunk * 16
-        rr = lax.broadcasted_iota(jnp.int32, (16, BLOCK, 256), 1)
-        lowest = jnp.where(at_left, 4, 0)
-        highest = jnp.where(at_right, 44, 48)
+        rr = lax.broadcasted_iota(jnp.int32, (4, BLOCK, 256), 1)
         up_row = jnp.where(at_top, 23, -1)
         down_row = jnp.where(at_bottom, 16, -1)
-        inside = (blk >= lowest) & (blk < highest) & (rr != up_row) & (rr != down_row)
-        total = rounded(jnp.where(inside, total, 0.0))
-        for slot, shift in enumerate((1, 0, BLOCK - 1)):
-            moved = pltpu.roll(total, shift, axis=1) if shift else total
-            r3s[pl.ds(pl.multiple_of(chunk * 384 + 96, 32), 384), slot * 256 : (slot + 1) * 256] = moved.reshape(
-                384, 256
-            ).astype(BF)
-        return 0
-
-    lax.fori_loop(0, 3, three, 0)
+        inside_rows = (rr != up_row) & (rr != down_row)
+        for n, c in enumerate(cols):
+            at = pl.ds(pl.multiple_of(c * 96 + 96, 32), 96)
+            piece = xs[at, :] + (total[n * 96 : n * 96 + 96] + bias3)
+            outside = jnp.logical_or(jnp.logical_and(at_left, c == 0), jnp.logical_and(at_right, c == 11))
+            inside = inside_rows & (rr >= jnp.where(outside, BLOCK, 0))
+            piece = rounded(jnp.where(inside, piece.reshape(4, BLOCK, 256), 0.0))
+            for slot, shift in enumerate((1, 0, BLOCK - 1)):
+                moved = pltpu.roll(piece, shift, axis=1) if shift else piece
+                r3s[at, slot * 256 : (slot + 1) * 256] = moved.reshape(96, 256).astype(BF)
+
+    def own_three(i, _):
+        three([2 + 4 * i + n for n in range(4)])
+        return 0
 
     bias_u = bu[...].reshape(1, C4)
     bias_u = jnp.concatenate([widen(bias_u, 128)] * 2, 1)
@@ -363,8 +360,6 @@
             )
             s4[py, pl.ds(pl.multiple_of(chunk * 384, 128), 384), :] = total + bias_u
         return 0
-
-    lax.fori_loop(0, 3, upsample, 0)
 
     gain4 = widen(g4[...].reshape(1, C4), 128)
 
@@ -395,7 +390,21 @@
                 )
         return 0
 
-    lax.fori_loop(0, 12, four_in, 0)
+    arrive(copies[:2])
+    for je in range(2, 2 + COLS):
+        edges(je)
+    lax.fori_loop(0, COLS, own_build, 0)
+    lax.fori_loop(0, 2, own_three, 0)
+    upsample(1, 0)
+    lax.fori_loop(4, 8, four_in, 0)
+
+    arrive(copies[2:])
+    for je in (0, 1, 2 + COLS, 3 + COLS):
+        edges(je)
+    lax.fori_loop(0, 4, side_build, 0)
+    three([0, 1, 10, 11])
+    lax.fori_loop(0, 2, lambda i, _: upsample(2 * i, 0), 0)
+    lax.fori_loop(0, 8, lambda i, _: four_in(i + i // 4 * 4, 0), 0)
 
     edge_q = X_LANES + P_LANES
     qext[0:32, 0:256] = keep(ql[...], at_left)

time: 34.1 us -> 35.3 us (1.035)
  Pallas kernels: 32.1 us -> 33.3 us
    pallas_call x1, Pallas kernels: 32.1 us -> 33.3 us  [shards(): pl.pallas_call(functools.partial(kernel, sizes), out_shape=jax.ShapeDtype...]
where the time goes in v3:
time: 35.3 us; the launch traced here: 35.2 us
  Pallas kernels  33.3 us (94%)
  local copies, waits for them, and re-layouts  1.84 us (5%)
    pallas_call x1, Pallas kernels, shards(): pl.pallas_call(functools.partial(kernel, sizes), out_shape=jax.ShapeDtype...  33.3 us
    unnamed x1, local copies, waits for them, and re-layouts  1.84 us

profile of v3, /device:TPU:1, one launch (start us, length us, event | category | flops | bytes accessed | tf_op | source)
XLA Modules:
  0.0 35.2 jit_solution(2292156118699275083)
XLA Ops:
  0.0 33.3 %decode.1 = bf16[32,7680]{1,0:T(8,128)(2,1)} custom-call(bf16[16,7680]{1,0:T(8,128)(2,1)} %x_hbm.1, bf16[16,3840]{1,0:T(8,128)(2,1)} %p_hbm.1, bf16[32,3840]{1,0:T(8,128)(2,1)} %q_hbm.1, bf16[27,36864]{1,0:T(8,128)(2,1)} %w3_hbm.1, bf16[9,18432]{1,0:T(8,128)(2,1)} %wu_hbm.1, bf16[27,9216]{1,0:T(8,128)(2,1)} %w4_hbm.1, f32[192]{0:T(256)} %g3_hbm.1, ...), custom_call_target="tpu_custom_call" | custom-call | tf_op jit(solution)/shard_map/decode/pallas_call | solution.py:530
  33.3 1.8 %copy.13 = bf16[32,7680]{1,0:T(8,128)(2,1)} copy(bf16[32,7680]{1,0:T(8,128)(2,1)} %decode.1) | data formatting | bytes 983040

commit v4 on v2

--- a/solution.py
+++ b/solution.py
@@ -312,8 +312,8 @@
         place(je, jnp.concatenate([main, edge], 1))
         return 0
 
-    lax.fori_loop(0, 4, side_build, 0)
-    lax.fori_loop(0, COLS, own_build, 0)
+    lax.fori_loop(0, 4, side_build, 0, unroll=4)
+    lax.fori_loop(0, COLS, own_build, 0, unroll=5)
 
     def three(chunk, _):
         parts = []
@@ -347,7 +347,7 @@
             ).astype(BF)
         return 0
 
-    lax.fori_loop(0, 3, three, 0)
+    lax.fori_loop(0, 3, three, 0, unroll=3)
 
     bias_u = bu[...].reshape(1, C4)
     bias_u = jnp.concatenate([widen(bias_u, 128)] * 2, 1)
@@ -364,7 +364,7 @@
             s4[py, pl.ds(pl.multiple_of(chunk * 384, 128), 384), :] = total + bias_u
         return 0
 
-    lax.fori_loop(0, 3, upsample, 0)
+    lax.fori_loop(0, 3, upsample, 0, unroll=3)
 
     gain4 = widen(g4[...].reshape(1, C4), 128)
 
@@ -395,7 +395,7 @@
                 )
         return 0
 
-    lax.fori_loop(0, 12, four_in, 0)
+    lax.fori_loop(0, 12, four_in, 0, unroll=4)
 
     edge_q = X_LANES + P_LANES
     qext[0:32, 0:256] = keep(ql[...], at_left)
@@ -461,7 +461,7 @@
                     outs[(chunk * 5 + x) * 3 + tile, pl.ds(py, 16, stride=2), :] = line[:, tile * 128 : tile * 128 + 128]
         return 0
 
-    lax.fori_loop(0, 4, four, 0)
+    lax.fori_loop(0, 4, four, 0, unroll=2)
     for copy, sends, _gets in copies:
 
         @pl.when(sends)

time: 34.1 us -> 31.7 us (0.930)
  Pallas kernels: 32.1 us -> 29.8 us
    pallas_call x1, Pallas kernels: 32.1 us -> 29.8 us  [shards(): pl.pallas_call(functools.partial(kernel, sizes), out_shape=jax.ShapeDtype...]
where the time goes in v4:
time: 31.7 us; the launch traced here: 31.6 us
  Pallas kernels  29.8 us (94%)
  local copies, waits for them, and re-layouts  1.84 us (6%)
    pallas_call x1, Pallas kernels, shards(): pl.pallas_call(functools.partial(kernel, sizes), out_shape=jax.ShapeDtype...  29.8 us
    unnamed x1, local copies, waits for them, and re-layouts  1.84 us

profile of v4, /device:TPU:1, one launch (start us, length us, event | category | flops | bytes accessed | tf_op | source)
XLA Modules:
  0.0 31.6 jit_solution(17894044655349284536)
XLA Ops:
  0.0 29.8 %decode.1 = bf16[32,7680]{1,0:T(8,128)(2,1)} custom-call(bf16[16,7680]{1,0:T(8,128)(2,1)} %x_hbm.1, bf16[16,3840]{1,0:T(8,128)(2,1)} %p_hbm.1, bf16[32,3840]{1,0:T(8,128)(2,1)} %q_hbm.1, bf16[27,36864]{1,0:T(8,128)(2,1)} %w3_hbm.1, bf16[9,18432]{1,0:T(8,128)(2,1)} %wu_hbm.1, bf16[27,9216]{1,0:T(8,128)(2,1)} %w4_hbm.1, f32[192]{0:T(256)} %g3_hbm.1, ...), custom_call_target="tpu_custom_call" | custom-call | tf_op jit(solution)/shard_map/decode/pallas_call | solution.py:521
  29.8 1.8 %copy.13 = bf16[32,7680]{1,0:T(8,128)(2,1)} copy(bf16[32,7680]{1,0:T(8,128)(2,1)} %decode.1) | data formatting | bytes 983040
